TPU v7x, 32 devices: a whole 2x2x4 slice. The times are simulated.
32 devices in a mesh: group: 4 (over z), tensor: 4 (over y, core), role: 2 (over x).
Axes of the slice: x: 2, y: 2, z: 4, core: 2. Of those that a mesh axis runs over, the one named last changes fastest.
Arguments:
- queries: bfloat16 [4096, 4096], P(('group', 'role'), 'tensor'), may hold values from -8 to 8
- keys_values: bfloat16 [2, 4096, 1024], P(None, ('group', 'role')), may hold values from -8 to 8
- doc_ids: int32 [4096], P(('group', 'role')), may hold values from 0 to 15, never falling along the last dimension, each value on 1 to 1024 neighbouring positions
Outputs:
- attended: bfloat16 [4096, 4096], P(('group', 'role'), 'tensor')
All inputs are finite; a program needn't handle non-finite values.
Results may differ from a plain program's by a relative error of at most 0.0036.
Values may be sent and summed in bfloat16 or wider, within the bound.
A program may use at most 64 MiB of HBM per device.

v0:
```python
import math

import jax
import jax.numpy as jnp
from jax import lax
from jax.sharding import PartitionSpec as P

HEADS = 32
KV_HEADS = 8
HD = 128


def absorb_keys(running, scores, visible, values, pattern):
    largest, totals, summed = running
    masked = jnp.where(visible, scores, -1e30)
    newest = jnp.maximum(largest, jnp.max(masked, axis=-1))
    factor = jnp.exp(largest - newest)
    weights = jnp.where(visible, jnp.exp(masked - newest[..., None]), 0.0)
    totals = totals * factor + jnp.sum(weights, axis=-1)
    rounded = weights.astype(jnp.bfloat16)
    summed = summed * factor[..., None] + jnp.einsum(
        pattern, rounded, values, preferred_element_type=jnp.float32
    )
    return (newest, totals, summed)


def head_attention(queries, keys_values, doc_ids):
    tok_rows, width_here = queries.shape
    role_index = lax.axis_index("role")
    tensor_index = lax.axis_index("tensor")
    heads_here = width_here // HD
    group_width = HEADS // KV_HEADS
    scaling = 1.0 / math.sqrt(HD)
    kv_count = max(1, heads_here // group_width)
    share = heads_here // kv_count
    first_kv = tensor_index * heads_here // group_width
    own_kv = lax.dynamic_slice_in_dim(keys_values, first_kv * HD, kv_count * HD, 2)[None]
    local_q = queries.reshape(tok_rows, kv_count, share, HD)
    query_pos = role_index * tok_rows + jnp.arange(tok_rows, dtype=jnp.int32)
    row_steps = jnp.arange(tok_rows, dtype=jnp.int32)
    start_state = (
        jnp.full((tok_rows, kv_count, share), -1e30, jnp.float32),
        jnp.zeros((tok_rows, kv_count, share), jnp.float32),
        jnp.zeros((tok_rows, kv_count, share, HD), jnp.float32),
    )
    kv_piece = lax.all_gather(own_kv, "role", axis=0, tiled=True)
    id_piece = lax.all_gather(doc_ids[None], "role", axis=0, tiled=True)

    def one_block(entry, state):

        def take(state_in):
            block = lax.dynamic_index_in_dim(kv_piece, entry, 0, keepdims=False)
            key_ids = lax.dynamic_index_in_dim(id_piece, entry, 0, keepdims=False)
            key_side = block[0].reshape(tok_rows, kv_count, HD)
            value_side = block[1].reshape(tok_rows, kv_count, HD)
            scores = (
                jnp.einsum("qcgd,kcd->qcgk", local_q, key_side, preferred_element_type=jnp.float32)
                * scaling
            )
            key_pos = entry * tok_rows + row_steps
            visible = (key_pos[None, :] <= query_pos[:, None]) & (
                key_ids[None, :] == doc_ids[:, None]
            )
            return absorb_keys(
                state_in, scores, visible[:, None, None, :], value_side, "qcgk,kcd->qcgd"
            )

        def keep(state_in):
            return state_in

        return lax.cond(entry <= role_index, take, keep, state)

    largest, totals, summed = lax.fori_loop(0, kv_piece.shape[0], one_block, start_state)
    return (summed / totals[..., None]).astype(jnp.bfloat16).reshape(tok_rows, width_here)


def per_device(queries, keys_values, doc_ids):
    attended = head_attention(queries, keys_values, doc_ids)
    return attended


def solution(mesh):
    in_specs = (
        P(("group", "role"), "tensor"),
        P(None, ("group", "role"), None),
        P(("group", "role")),
    )
    out_specs = P(("group", "role"), "tensor")
    return jax.shard_map(
        per_device, mesh=mesh, in_specs=in_specs, out_specs=out_specs, check_vma=False
    )
```

profile of v0, /device:TPU:6, one launch (start us, length us, event | category | flops | bytes accessed | tf_op | source)
XLA Modules:
  0.0 64.0 jit_solution(12343102273541048219)
XLA Ops:
  6.5 0.0 copy-start
  6.5 0.0 copy-start.3
  6.5 0.0 all-gather.5.cloned.1.call-start
  6.5 1.6 %copy-done = bf16[2,512,1024]{2,1,0:T(8,128)(2,1)S(1)} copy-done((bf16[2,512,1024]{2,1,0:T(8,128)(2,1)S(1)}, bf16[2,512,1024]{2,1,0:T(8,128)(2,1)}, u32[]{:S(2)}) %copy-start) | copy-done | bytes 2097176
  8.1 0.9 %constant_dynamic-slice_fusion.3 = bf16[2,512,256]{2,1,0:T(8,128)(2,1)} fusion(bf16[2,512,1024]{2,1,0:T(8,128)(2,1)S(1)} %copy-done, s32[]{:T(128)S(6)} %select_n.22), kind=kLoop, calls=%fused_computation.23 | loop fusion | bytes 1048580 | tf_op jit(solution)/shard_map/dynamic_slice | solution.py:37
  9.0 0.0 all-gather.5.cloned.1.call-update
  9.0 2.3 %copy.15 = bf16[512,1024]{0,1:T(8,128)(2,1)} copy(bf16[512,1024]{1,0:T(8,128)(2,1)} %param.7) | data formatting | bytes 2097152 | tf_op args[0]
  11.3 1.6 %copy.17 = bf16[512,2,4,128]{3,0,2,1:T(8,128)(2,1)S(1)} copy(bf16[512,2,4,128]{0,3,2,1:T(8,128)(2,1)} %bitcast.46) | data formatting | bytes 2097152
  12.9 4.5 %all-gather.2 = s32[2,1,512]{2,1,0:T(1,128)S(1)} all-gather(s32[1,1,512]{2,1,0:T(1,128)} %bitcast.54), channel_id=2, replica_groups=mesh['group'=4,'tensor'=4,'role'=2] {'role'}, dimensions={0}, use_global_device_ids=true | all-gather | bytes 6144 | tf_op jit(solution)/shard_map/all_gather | solution.py:47
  17.4 13.3 %all-gather.5.cloned.1.call-done = bf16[4,512,256]{2,1,0:T(8,128)(2,1)} async-done(((bf16[2,512,256]{2,1,0:T(8,128)(2,1)}), bf16[4,512,256]{2,1,0:T(8,128)(2,1)}) %all-gather.5.cloned.1.call-update) | async-done | bytes 1048592 | tf_op jit(solution)/shard_map/all_gather | solution.py:46
  30.7 2.3 %copy.16 = bf16[2,2,512,256]{2,3,1,0:T(8,128)(2,1)} copy(bf16[2,2,512,256]{3,2,1,0:T(8,128)(2,1)} %bitcast.49) | data formatting | bytes 2097152
  33.0 1.6 %broadcast_in_dim.43 = f32[512,2,4,128]{0,3,2,1:T(8,128)} broadcast(f32[]{:T(128)} %constant.57.clone.1), dimensions={} | broadcast | bytes 2097156 | tf_op jit(solution)/shard_map/broadcast_in_dim | solution.py:44
  34.6 0.0 copy-done.3
  34.6 19.3 %while.18 = (s32[]{:T(128)}, f32[512,2,4]{0,2,1:T(4,128)S(1)}, f32[512,2,4]{0,2,1:T(4,128)S(1)}, f32[512,2,4,128]{0,3,2,1:T(8,128)}, s32[]{:T(128)}, /*index=5*/...) while((s32[]{:T(128)}, f32[512,2,4]{0,2,1:T(4,128)S(1)}, ...), condition=%wide.region_5.6_spmd.clone, body=%wide.region_0.5_spmd.clone.sunk | while | flops 1102849024 | bytes 50092432 | solution.py:73
  34.7 9.6 %conditional.3 = ((f32[512,2,4]{0,2,1:T(4,128)S(1)}, f32[512,2,4]{0,2,1:T(4,128)S(1)}, f32[512,2,4,128]{0,3,2,1:T(8,128)})) conditional(s32[]{:T(128)} %convert_element_type.21, (f32[512,2,4]{0,2,1:T(4,128)S(1)}, f32[512,2,4]{0,2,1:T(4,128)S(1)}, f32[512,2,4,128]{0,3,2,1:T(8,128)}) %tuple.49, (s32[]{:T(128)}, s32[512]{0:T(512)S(1)}, s32[]{:T(128)}, ...), branch_computations={%region_1.1_spmd, %region_2.4_spmd} | conditional | flops 1102849024 | bytes 50090148 | solution.py:71
  34.7 0.3 compare_and_fusion
  35.0 1.1 %constant_dynamic-slice_fusion.1 = (bf16[1,1,512,256]{2,3,1,0:T(8,128)(2,1)S(1)}, bf16[1,1,512,256]{2,3,1,0:T(8,128)(2,1)S(1)}) fusion(bf16[2,2,512,256]{2,3,1,0:T(8,128)(2,1)} %get-tuple-element.214, s32[]{:T(128)S(6)} %select_n.16, s32[]{:T(128)S(6)} %add.58), kind=kLoop, calls=%fused_computation.16 | loop fusion | bytes 1048584 | tf_op jit(solution)/shard_map/while/body/eval_jaxpr/cond/branch_1_fun/slice | solution.py:55
  36.1 0.0 copy-start.1
  36.1 2.1 %fusion.4 = (f32[512,2,4]{0,2,1:T(4,128)S(1)}, f32[2,512,512,4]{2,1,3,0:T(8,128)S(1)}) fusion(pred[512,512]{0,1:T(8,128)(4,1)S(1)} %compare_and_fusion, bf16[512,2,128,1]{0,2,3,1:T(8,128)(2,1)S(1)} %bitcast.42, bf16[512,2,4,128]{3,0,2,1:T(8,128)(2,1)S(1)} %get-tuple-element.215), kind=kOutput, calls=%fused_computation.4 | convolution fusion | flops 543158272 | bytes 9977856 | tf_op jit(solution)/shard_map/while/body/eval_jaxpr/cond/branch_1_fun/qcgd,kcd->qcgk/dot_general | solution.py:57
  38.2 2.0 %fusion.6 = f32[512,2,4]{0,2,1:T(4,128)S(1)} fusion(f32[2,512,512,4]{2,1,3,0:T(8,128)S(1)} %get-tuple-element.312, f32[512,2,4]{0,2,1:T(4,128)S(1)} %max.2, pred[512,512]{0,1:T(8,128)(4,1)S(1)} %compare_and_fusion), kind=kLoop, calls=%fused_computation.6 | loop fusion | flops 10481664 | bytes 8683520 | tf_op jit(solution)/shard_map/while/body/eval_jaxpr/cond/branch_1_fun/reduce_sum | solution.py:19
  40.2 0.0 copy-done.1
  40.2 2.7 %bitcast_add_fusion = f32[512,2,4,128]{0,3,2,1:T(8,128)S(1)} fusion(f32[512,2,4,128]{0,3,2,1:T(8,128)S(1)} %copy-done.1, bf16[512,2,128,1]{0,2,3,1:T(8,128)(2,1)S(1)} %bitcast.44, f32[2,512,512,4]{2,1,3,0:T(8,128)S(1)} %get-tuple-element.312, f32[512,2,4]{0,2,1:T(4,128)S(1)} %max.2, pred[512,512]{0,1:T(8,128)(4,1)S(1)} %compare_and_fusion, ...), kind=kOutput, calls=%fused_computation.9 | convolution fusion | flops 548405248 | bytes 13139968 | tf_op jit(solution)/shard_map/while/body/eval_jaxpr/cond/branch_1_fun/qcgk,kcd->qcgd/dot_general | solution.py:21
  43.0 0.0 copy-start.2
  43.0 1.3 %copy-done.2 = f32[512,2,4,128]{0,3,2,1:T(8,128)} copy-done((f32[512,2,4,128]{0,3,2,1:T(8,128)}, f32[512,2,4,128]{0,3,2,1:T(8,128)S(1)}, u32[]{:S(2)}) %copy-start.2) | copy-done | bytes 2097176 | tf_op jit(solution)/shard_map/while/body/eval_jaxpr/cond
  44.3 9.6 %conditional.3 = ((f32[512,2,4]{0,2,1:T(4,128)S(1)}, f32[512,2,4]{0,2,1:T(4,128)S(1)}, f32[512,2,4,128]{0,3,2,1:T(8,128)})) conditional(s32[]{:T(128)} %convert_element_type.21, (f32[512,2,4]{0,2,1:T(4,128)S(1)}, f32[512,2,4]{0,2,1:T(4,128)S(1)}, f32[512,2,4,128]{0,3,2,1:T(8,128)}) %tuple.49, (s32[]{:T(128)}, s32[512]{0:T(512)S(1)}, s32[]{:T(128)}, ...), branch_computations={%region_1.1_spmd, %region_2.4_spmd} | conditional | flops 1102849024 | bytes 50090148 | solution.py:71
  44.3 0.3 compare_and_fusion
  44.6 1.1 %constant_dynamic-slice_fusion.1 = (bf16[1,1,512,256]{2,3,1,0:T(8,128)(2,1)S(1)}, bf16[1,1,512,256]{2,3,1,0:T(8,128)(2,1)S(1)}) fusion(bf16[2,2,512,256]{2,3,1,0:T(8,128)(2,1)} %get-tuple-element.214, s32[]{:T(128)S(6)} %select_n.16, s32[]{:T(128)S(6)} %add.58), kind=kLoop, calls=%fused_computation.16 | loop fusion | bytes 1048584 | tf_op jit(solution)/shard_map/while/body/eval_jaxpr/cond/branch_1_fun/slice | solution.py:55
  45.7 0.0 copy-start.1
  45.7 2.1 %fusion.4 = (f32[512,2,4]{0,2,1:T(4,128)S(1)}, f32[2,512,512,4]{2,1,3,0:T(8,128)S(1)}) fusion(pred[512,512]{0,1:T(8,128)(4,1)S(1)} %compare_and_fusion, bf16[512,2,128,1]{0,2,3,1:T(8,128)(2,1)S(1)} %bitcast.42, bf16[512,2,4,128]{3,0,2,1:T(8,128)(2,1)S(1)} %get-tuple-element.215), kind=kOutput, calls=%fused_computation.4 | convolution fusion | flops 543158272 | bytes 9977856 | tf_op jit(solution)/shard_map/while/body/eval_jaxpr/cond/branch_1_fun/qcgd,kcd->qcgk/dot_general | solution.py:57
  47.8 2.0 %fusion.6 = f32[512,2,4]{0,2,1:T(4,128)S(1)} fusion(f32[2,512,512,4]{2,1,3,0:T(8,128)S(1)} %get-tuple-element.312, f32[512,2,4]{0,2,1:T(4,128)S(1)} %max.2, pred[512,512]{0,1:T(8,128)(4,1)S(1)} %compare_and_fusion), kind=kLoop, calls=%fused_computation.6 | loop fusion | flops 10481664 | bytes 8683520 | tf_op jit(solution)/shard_map/while/body/eval_jaxpr/cond/branch_1_fun/reduce_sum | solution.py:19
  49.9 0.0 copy-done.1
  49.9 2.7 %bitcast_add_fusion = f32[512,2,4,128]{0,3,2,1:T(8,128)S(1)} fusion(f32[512,2,4,128]{0,3,2,1:T(8,128)S(1)} %copy-done.1, bf16[512,2,128,1]{0,2,3,1:T(8,128)(2,1)S(1)} %bitcast.44, f32[2,512,512,4]{2,1,3,0:T(8,128)S(1)} %get-tuple-element.312, f32[512,2,4]{0,2,1:T(4,128)S(1)} %max.2, pred[512,512]{0,1:T(8,128)(4,1)S(1)} %compare_and_fusion, ...), kind=kOutput, calls=%fused_computation.9 | convolution fusion | flops 548405248 | bytes 13139968 | tf_op jit(solution)/shard_map/while/body/eval_jaxpr/cond/branch_1_fun/qcgk,kcd->qcgd/dot_general | solution.py:21
  52.6 0.0 copy-start.2
  52.6 1.3 %copy-done.2 = f32[512,2,4,128]{0,3,2,1:T(8,128)} copy-done((f32[512,2,4,128]{0,3,2,1:T(8,128)}, f32[512,2,4,128]{0,3,2,1:T(8,128)S(1)}, u32[]{:S(2)}) %copy-start.2) | copy-done | bytes 2097176 | tf_op jit(solution)/shard_map/while/body/eval_jaxpr/cond
  53.9 1.9 %divide_convert_fusion = bf16[512,2,4,128]{0,3,2,1:T(8,128)(2,1)S(1)} fusion(f32[512,2,4,128]{0,3,2,1:T(8,128)} %get-tuple-element.235, f32[512,2,4]{0,2,1:T(4,128)S(1)} %get-tuple-element.236), kind=kLoop, calls=%fused_computation.21 | loop fusion | flops 1048576 | bytes 3162112 | tf_op jit(solution)/shard_map/convert_element_type | solution.py:74
  55.8 1.3 %copy.24 = bf16[512,1024]{1,0:T(8,128)(2,1)} copy(bf16[512,1024]{0,1:T(8,128)(2,1)S(1)} %bitcast.45) | data formatting | bytes 2097152 | tf_op jit(solution)/shard_map/reshape | solution.py:74
  (15 shorter events, 0.1 us)
Async XLA Ops:
  6.5 1.6 %copy-start = (bf16[2,512,1024]{2,1,0:T(8,128)(2,1)S(1)}, bf16[2,512,1024]{2,1,0:T(8,128)(2,1)}, u32[]{:S(2)}) copy-start(bf16[2,512,1024]{2,1,0:T(8,128)(2,1)} %param.8) | copy-start | bytes 6291460
  6.5 28.1 %copy-start.3 = (s32[512]{0:T(512)S(1)}, s32[512]{0:T(512)}, u32[]{:S(2)}) copy-start(s32[512]{0:T(512)} %param.9) | copy-start | bytes 6148
  6.5 24.2 %all-gather.5.cloned.1.call-start = ((), (), s32[]{:S(2)}) async-start(), calls=%async_computation | async-start | bytes 1572864 | tf_op jit(solution)/shard_map/all_gather | solution.py:46
  36.1 4.2 %copy-start.1 = (f32[512,2,4,128]{0,3,2,1:T(8,128)S(1)}, f32[512,2,4,128]{0,3,2,1:T(8,128)}, u32[]{:S(2)}) copy-start(f32[512,2,4,128]{0,3,2,1:T(8,128)} %get-tuple-element.217) | copy-start | bytes 6291460 | tf_op jit(solution)/shard_map/while/body/eval_jaxpr/cond
  43.0 1.3 %copy-start.2 = (f32[512,2,4,128]{0,3,2,1:T(8,128)}, f32[512,2,4,128]{0,3,2,1:T(8,128)S(1)}, u32[]{:S(2)}) copy-start(f32[512,2,4,128]{0,3,2,1:T(8,128)S(1)} %bitcast_add_fusion) | copy-start | bytes 6291460 | tf_op jit(solution)/shard_map/while/body/eval_jaxpr/cond
  45.7 4.2 %copy-start.1 = (f32[512,2,4,128]{0,3,2,1:T(8,128)S(1)}, f32[512,2,4,128]{0,3,2,1:T(8,128)}, u32[]{:S(2)}) copy-start(f32[512,2,4,128]{0,3,2,1:T(8,128)} %get-tuple-element.217) | copy-start | bytes 6291460 | tf_op jit(solution)/shard_map/while/body/eval_jaxpr/cond
  52.6 1.3 %copy-start.2 = (f32[512,2,4,128]{0,3,2,1:T(8,128)}, f32[512,2,4,128]{0,3,2,1:T(8,128)S(1)}, u32[]{:S(2)}) copy-start(f32[512,2,4,128]{0,3,2,1:T(8,128)S(1)} %bitcast_add_fusion) | copy-start | bytes 6291460 | tf_op jit(solution)/shard_map/while/body/eval_jaxpr/cond
Sparse Core Ops, SparseCore 0:
  9.2 21.5 all-gather.4
where the time goes:
time: 64.2 us; the launch traced here: 64 us
  local copies, waits for them, and re-layouts  16.4 us (26%)
  between operations  13.4 us (21%)
  waiting for transfers between devices  13.3 us (21%)
  matrix products  9.54 us (15%)
  other arithmetic  6.56 us (10%)
  blocking collectives  4.5 us (7%)
    all_gather x1, waiting for transfers between devices, head_attention(): kv_piece = lax.all_gather(own_kv, 'role', axis=0, tiled=True)  13.3 us
    unnamed x8, local copies, waits for them, and re-layouts  7.75 us
    dot_general x2, matrix products, absorb_keys(): jnp.einsum(pattern, rounded, values, preferred_element_type=jnp.float32)  5.43 us
    all_gather x1, blocking collectives, head_attention(): id_piece = lax.all_gather(doc_ids[None], 'role', axis=0, tiled=True)  4.5 us
    dot_general x2, matrix products, take(): jnp.einsum('qcgd,kcd->qcgk', local_q, key_side, preferred_element_type=jn...  4.1 us
    reduce_sum x2, other arithmetic, absorb_keys(): totals = totals * factor + jnp.sum(weights, axis=-1)  4.09 us
    cond x10, local copies, waits for them, and re-layouts  2.68 us
    slice x2, local copies, waits for them, and re-layouts, take(): value_side = block[1].reshape(tok_rows, kv_count, HD)  2.14 us
  transfers between devices with their start and end apart: 1, of which 1 were waited for; matrix products, arithmetic and copies ran while one was open for 6% of the time, Pallas kernels for 0%

commit v1 on v0

v1 whole, which is shorter than its diff:
```python
import functools
import math

import jax
import jax.numpy as jnp
from jax import lax
from jax.experimental import pallas as pl
from jax.experimental.pallas import tpu as pltpu
from jax.sharding import PartitionSpec as P

HD = 128
TILE = 128
HIDDEN = -1e30
MESH = pl.DeviceIdType.MESH


def dot_t(a, b):
    return lax.dot_general(a, b, (((1,), (1,)), ((), ())), preferred_element_type=jnp.float32)


def dot(a, b):
    return lax.dot_general(a, b, (((1,), (0,)), ((), ())), preferred_element_type=jnp.float32)


def kernel(
    n, kvc, share, group_width, q_hbm, kv_hbm, ids_ref, out_hbm,
    q, k_own, v_own, k_in, v_in, ids_in, ids_col, bias, weights, acc, top, total, out_buf,
    q_sem, k_sem, v_sem, out_sem, ids_send, ids_recv, k_send, k_recv, v_send, v_recv,
):
    rows = q_hbm.shape[0]
    heads = kvc * share
    tiles = rows // TILE
    width = share * HD
    role = lax.axis_index("role")
    first_kv = lax.axis_index("tensor") * heads // group_width
    rate = math.log2(math.e) / math.sqrt(HD)

    barrier = pltpu.get_barrier_semaphore()
    for k in range(1, n):
        pl.semaphore_signal(
            barrier, inc=1, device_id={"role": lax.rem(role + k, n)}, device_id_type=MESH
        )

    def side(which, c):
        return kv_hbm.at[which, :, pl.ds(pl.multiple_of((first_kv + c) * HD, HD), HD)]

    def q_copy(c):
        cols = slice(c * width, (c + 1) * width)
        return pltpu.make_async_copy(q_hbm.at[:, cols], q.at[:, cols], q_sem.at[c])

    def k_copy(c):
        return pltpu.make_async_copy(side(0, c), k_own.at[c], k_sem.at[c])

    def v_copy(c):
        return pltpu.make_async_copy(side(1, c), v_own.at[c], v_sem.at[c])

    def out_copy(c):
        cols = slice(c * width, (c + 1) * width)
        return pltpu.make_async_copy(out_buf.at[:, cols], out_hbm.at[:, cols], out_sem.at[c])

    def remote(src, dst, send, recv, k):
        return pltpu.make_async_remote_copy(
            src_ref=src, dst_ref=dst, send_sem=send, recv_sem=recv,
            device_id={"role": lax.rem(role + k, n)}, device_id_type=MESH,
        )

    def ids_remote(k):
        return remote(ids_ref, ids_in.at[k - 1], ids_send.at[k - 1], ids_recv.at[k - 1], k)

    def k_remote(k, c):
        return remote(side(0, c), k_in.at[k - 1, c], k_send.at[k - 1, c], k_recv.at[k - 1, c], k)

    def v_remote(k, c):
        return remote(side(1, c), v_in.at[k - 1, c], v_send.at[k - 1, c], v_recv.at[k - 1, c], k)

    for c in range(kvc):
        q_copy(c).start()
        k_copy(c).start()
        v_copy(c).start()
    if n > 1:
        pl.semaphore_wait(barrier, n - 1)
    for k in range(1, n):

        @pl.when(role + k < n)
        def _():
            ids_remote(k).start()
            for c in range(kvc):
                k_remote(k, c).start()
            for c in range(kvc):
                v_remote(k, c).start()

    ids_row = ids_ref[...]
    ids_col[...] = jnp.transpose(jnp.broadcast_to(ids_row, (HD, rows)))

    def wide(part, times):
        return jnp.concatenate([part] * times, axis=1) if times > 1 else part

    for t in range(tiles):
        r = slice(t * TILE, (t + 1) * TILE)
        w = (t + 1) * TILE
        row_at = lax.broadcasted_iota(jnp.int32, (TILE, w), 0) + t * TILE
        col_at = lax.broadcasted_iota(jnp.int32, (TILE, w), 1)
        same = wide(ids_col[r, :], w // HD) == ids_row[:, :w]
        bias[r, :w] = jnp.where(same & (col_at <= row_at), 0.0, HIDDEN)

    def head_cols(h):
        return pl.ds(pl.multiple_of(h * HD, HD), HD)

    def own(c, j):
        h = c * share + j
        for t in range(tiles):
            r = slice(t * TILE, (t + 1) * TILE)
            w = (t + 1) * TILE
            s = dot_t(q[r, head_cols(h)], k_own[c, :w, :]) + bias[r, :w]
            largest = jnp.max(s, axis=1, keepdims=True)
            e = jnp.exp2((s - largest) * rate)
            top[h, r, :] = jnp.broadcast_to(largest, (TILE, HD))
            total[h, r, :] = jnp.broadcast_to(jnp.sum(e, axis=1, keepdims=True), (TILE, HD))
            acc[h, r, :] = dot(e.astype(jnp.bfloat16), v_own[c, :w, :])

    for c in range(kvc):
        q_copy(c).wait()
        k_copy(c).wait()
        v_copy(c).wait()
        lax.fori_loop(0, share, lambda j, carry: (own(c, j), carry)[1], 0)

    def weigh(k, c, j):
        h = c * share + j
        for t in range(tiles):
            r = slice(t * TILE, (t + 1) * TILE)
            s = dot_t(q[r, head_cols(h)], k_in[k - 1, c]) + bias[r, :]
            before = top[h, r, :]
            largest = jnp.maximum(before, jnp.max(s, axis=1, keepdims=True))
            e = jnp.exp2((s - wide(largest, rows // HD)) * rate)
            factor = jnp.exp2((before - largest) * rate)
            weights[h, r, :] = e.astype(jnp.bfloat16)
            top[h, r, :] = largest
            total[h, r, :] = total[h, r, :] * factor + jnp.sum(e, axis=1, keepdims=True)
            acc[h, r, :] = acc[h, r, :] * factor

    def add_values(k, c, j):
        h = c * share + j
        acc[h] = acc[h] + dot(weights[h], v_in[k - 1, c])

    def finish_values(k, c, j):
        h = c * share + j
        summed = acc[h] + dot(weights[h], v_in[k - 1, c])
        out_buf[:, head_cols(h)] = (summed / total[h]).astype(jnp.bfloat16)

    def finish_own(c, j):
        h = c * share + j
        out_buf[:, head_cols(h)] = (acc[h] / total[h]).astype(jnp.bfloat16)

    def each(body):
        lax.fori_loop(0, share, lambda j, carry: (body(j), carry)[1], 0)

    for k in range(1, n):

        @pl.when(role >= k)
        def _():
            ids_remote(k).wait_recv()
            same = wide(ids_col[...], rows // HD) == ids_in[k - 1]
            bias[...] = jnp.where(same, 0.0, HIDDEN)
            for c in range(kvc):
                k_remote(k, c).wait_recv()
                each(functools.partial(weigh, k, c))
            for c in range(kvc):
                v_remote(k, c).wait_recv()

                @pl.when(role > k)
                def _():
                    each(functools.partial(add_values, k, c))

                @pl.when(role == k)
                def _():
                    each(functools.partial(finish_values, k, c))
                    out_copy(c).start()

    @pl.when(role == 0)
    def _():
        for c in range(kvc):
            each(functools.partial(finish_own, c))
            out_copy(c).start()

    for c in range(kvc):
        out_copy(c).wait()
    for k in range(1, n):

        @pl.when(role + k < n)
        def _():
            ids_remote(k).wait_send()
            for c in range(kvc):
                k_remote(k, c).wait_send()
                v_remote(k, c).wait_send()


def solution(mesh):
    n = mesh.shape["role"]
    parts = mesh.shape["tensor"]

    def per_device(queries, keys_values, doc_ids):
        rows, width_here = queries.shape
        heads = width_here // HD
        group_width = heads * parts // (keys_values.shape[2] // HD)
        kvc = max(1, heads // group_width)
        share = heads // kvc
        past = max(1, n - 1)
        bf16, f32, i32 = jnp.bfloat16, jnp.float32, jnp.int32
        dma = pltpu.SemaphoreType.DMA
        return pl.pallas_call(
            functools.partial(kernel, n, kvc, share, group_width),
            out_shape=jax.ShapeDtypeStruct((rows, width_here), bf16),
            in_specs=[
                pl.BlockSpec(memory_space=pl.ANY),
                pl.BlockSpec(memory_space=pl.ANY),
                pl.BlockSpec(memory_space=pltpu.VMEM),
            ],
            out_specs=pl.BlockSpec(memory_space=pl.ANY),
            scratch_shapes=[
                pltpu.VMEM((rows, width_here), bf16),
                pltpu.VMEM((kvc, rows, HD), bf16),
                pltpu.VMEM((kvc, rows, HD), bf16),
                pltpu.VMEM((past, kvc, rows, HD), bf16),
                pltpu.VMEM((past, kvc, rows, HD), bf16),
                pltpu.VMEM((past, 1, rows), i32),
                pltpu.VMEM((rows, HD), i32),
                pltpu.VMEM((rows, rows), f32),
                pltpu.VMEM((heads, rows, rows), bf16),
                pltpu.VMEM((heads, rows, HD), f32),
                pltpu.VMEM((heads, rows, HD), f32),
                pltpu.VMEM((heads, rows, HD), f32),
                pltpu.VMEM((rows, width_here), bf16),
                dma((kvc,)), dma((kvc,)), dma((kvc,)), dma((kvc,)),
                dma((past,)), dma((past,)),
                dma((past, kvc)), dma((past, kvc)), dma((past, kvc)), dma((past, kvc)),
            ],
            compiler_params=pltpu.CompilerParams(
                collective_id=0, has_side_effects=True, vmem_limit_bytes=40 << 20
            ),
        )(queries, keys_values, doc_ids[None])

    return jax.shard_map(
        per_device,
        mesh=mesh,
        in_specs=(
            P(("group", "role"), "tensor"),
            P(None, ("group", "role"), None),
            P(("group", "role")),
        ),
        out_specs=P(("group", "role"), "tensor"),
        check_vma=False,
    )
```

time: 64.2 us -> 21.8 us (0.34)
  Pallas kernels: 0 us -> 17.1 us
  between operations: 13.4 us -> 0.01 us
  waiting for transfers between devices: 13.3 us -> 0 us
  local copies, waits for them, and re-layouts: 16.4 us -> 4.47 us
  matrix products: 9.54 us -> 0 us
  other arithmetic: 6.56 us -> 0 us
  blocking collectives: 4.5 us -> 0 us
    pallas_call x0 -> x1, Pallas kernels: none -> 17.1 us  [per_device(): pl.pallas_call(functools.partial(kernel, n, kvc, share, group_width), out...]
    all_gather x1 -> x0, waiting for transfers between devices: 13.3 us -> none  [head_attention(): kv_piece = lax.all_gather(own_kv, 'role', axis=0, tiled=True)]
    dot_general x4 -> x0, matrix products: 9.54 us -> none  [the longest x2 5.43 us: absorb_keys(): jnp.einsum(pattern, rounded, values, preferred_element_type=jnp.float32)]
    all_gather x1 -> x0, blocking collectives: 4.5 us -> none  [head_attention(): id_piece = lax.all_gather(doc_ids[None], 'role', axis=0, tiled=True)]
    reduce_sum x2 -> x0, other arithmetic: 4.09 us -> none  [absorb_keys(): totals = totals * factor + jnp.sum(weights, axis=-1)]
    unnamed x8 -> x7, local copies, waits for them, and re-layouts: 7.75 us -> 4.47 us
    cond x10 -> x0, local copies, waits for them, and re-layouts: 2.68 us -> none
    slice x2 -> x0, local copies, waits for them, and re-layouts: 2.14 us -> none  [take(): value_side = block[1].reshape(tok_rows, kv_count, HD)]
  transfers between devices with their start and end apart: 1 -> 0, of which waited for: 1 -> 0; matrix products, arithmetic and copies ran while one was open for 6% -> 0% of each run, Pallas kernels for 0% -> 0%
where the time goes in v1:
time: 21.8 us; the launch traced here: 21.6 us
  Pallas kernels  17.1 us (78%)
  local copies, waits for them, and re-layouts  4.47 us (21%)
    pallas_call x1, Pallas kernels, per_device(): pl.pallas_call(functools.partial(kernel, n, kvc, share, group_width), out...  17.1 us
    unnamed x7, local copies, waits for them, and re-layouts  4.47 us

profile of v1, /device:TPU:6, one launch (start us, length us, event | category | flops | bytes accessed | tf_op | source)
XLA Modules:
  0.0 21.6 jit_solution(4074861421889542514)
XLA Ops:
  0.0 0.0 copy-start
  0.0 1.6 %copy-done = bf16[2,512,1024]{2,1,0:T(8,128)(2,1)S(1)} copy-done((bf16[2,512,1024]{2,1,0:T(8,128)(2,1)S(1)}, bf16[2,512,1024]{2,1,0:T(8,128)(2,1)}, u32[]{:S(2)}) %copy-start) | copy-done | bytes 2097176
  1.6 0.0 copy-start.1
  1.6 1.2 %copy-done.1 = bf16[512,1024]{1,0:T(8,128)(2,1)S(1)} copy-done((bf16[512,1024]{1,0:T(8,128)(2,1)S(1)}, bf16[512,1024]{1,0:T(8,128)(2,1)}, u32[]{:S(2)}) %copy-start.1) | copy-done | bytes 1048600
  2.8 0.0 copy-start.2
  2.8 0.7 %copy-done.2 = s32[512]{0:T(512)S(1)} copy-done((s32[512]{0:T(512)S(1)}, s32[512]{0:T(512)}, u32[]{:S(2)}) %copy-start.2) | copy-done | bytes 2072
  3.5 17.1 %shard_map.37 = bf16[512,1024]{1,0:T(8,128)(2,1)S(1)} custom-call(bf16[512,1024]{1,0:T(8,128)(2,1)S(1)} %copy-done.1, bf16[2,512,1024]{2,1,0:T(8,128)(2,1)S(1)} %copy-done, s32[1,512]{1,0:T(1,128)S(1)} %bitcast.1), custom_call_target="tpu_custom_call" | custom-call | tf_op jit(solution)/shard_map/pallas_call | solution.py:210
  20.6 1.0 %copy.5 = bf16[512,1024]{1,0:T(8,128)(2,1)} copy(bf16[512,1024]{1,0:T(8,128)(2,1)S(1)} %shard_map.37) | data formatting | bytes 2097152
Async XLA Ops:
  0.0 1.6 %copy-start = (bf16[2,512,1024]{2,1,0:T(8,128)(2,1)S(1)}, bf16[2,512,1024]{2,1,0:T(8,128)(2,1)}, u32[]{:S(2)}) copy-start(bf16[2,512,1024]{2,1,0:T(8,128)(2,1)} %kv_hbm.1) | copy-start | bytes 6291460
  1.6 1.2 %copy-start.1 = (bf16[512,1024]{1,0:T(8,128)(2,1)S(1)}, bf16[512,1024]{1,0:T(8,128)(2,1)}, u32[]{:S(2)}) copy-start(bf16[512,1024]{1,0:T(8,128)(2,1)} %q_hbm.1) | copy-start | bytes 3145732
  2.8 0.7 %copy-start.2 = (s32[512]{0:T(512)S(1)}, s32[512]{0:T(512)}, u32[]{:S(2)}) copy-start(s32[512]{0:T(512)} %param.5) | copy-start | bytes 6148

commit v2 on v1

--- a/solution.py
+++ b/solution.py
@@ -23,9 +23,9 @@
 
 
 def kernel(
-    n, kvc, share, group_width, q_hbm, kv_hbm, ids_ref, out_hbm,
-    q, k_own, v_own, k_in, v_in, ids_in, ids_col, bias, weights, acc, top, total, out_buf,
-    q_sem, k_sem, v_sem, out_sem, ids_send, ids_recv, k_send, k_recv, v_send, v_recv,
+    n, kvc, share, group_width, q_hbm, kv_hbm, ids_hbm, out_hbm,
+    q, k_own, v_own, k_in, v_in, ids_own, ids_in, ids_col, bias, weights, acc, top, total, out_buf,
+    ids_sem, q_sem, k_sem, v_sem, out_sem, ids_send, ids_recv, k_send, k_recv, v_send, v_recv,
 ):
     rows = q_hbm.shape[0]
     heads = kvc * share
@@ -65,7 +65,7 @@
         )
 
     def ids_remote(k):
-        return remote(ids_ref, ids_in.at[k - 1], ids_send.at[k - 1], ids_recv.at[k - 1], k)
+        return remote(ids_hbm, ids_in.at[k - 1], ids_send.at[k - 1], ids_recv.at[k - 1], k)
 
     def k_remote(k, c):
         return remote(side(0, c), k_in.at[k - 1, c], k_send.at[k - 1, c], k_recv.at[k - 1, c], k)
@@ -73,6 +73,8 @@
     def v_remote(k, c):
         return remote(side(1, c), v_in.at[k - 1, c], v_send.at[k - 1, c], v_recv.at[k - 1, c], k)
 
+    ids_copy = pltpu.make_async_copy(ids_hbm, ids_own, ids_sem)
+    ids_copy.start()
     for c in range(kvc):
         q_copy(c).start()
         k_copy(c).start()
@@ -89,7 +91,8 @@
             for c in range(kvc):
                 v_remote(k, c).start()
 
-    ids_row = ids_ref[...]
+    ids_copy.wait()
+    ids_row = ids_own[...]
     ids_col[...] = jnp.transpose(jnp.broadcast_to(ids_row, (HD, rows)))
 
     def wide(part, times):
@@ -213,7 +216,7 @@
             in_specs=[
                 pl.BlockSpec(memory_space=pl.ANY),
                 pl.BlockSpec(memory_space=pl.ANY),
-                pl.BlockSpec(memory_space=pltpu.VMEM),
+                pl.BlockSpec(memory_space=pl.ANY),
             ],
             out_specs=pl.BlockSpec(memory_space=pl.ANY),
             scratch_shapes=[
@@ -222,6 +225,7 @@
                 pltpu.VMEM((kvc, rows, HD), bf16),
                 pltpu.VMEM((past, kvc, rows, HD), bf16),
                 pltpu.VMEM((past, kvc, rows, HD), bf16),
+                pltpu.VMEM((1, rows), i32),
                 pltpu.VMEM((past, 1, rows), i32),
                 pltpu.VMEM((rows, HD), i32),
                 pltpu.VMEM((rows, rows), f32),
@@ -230,14 +234,18 @@
                 pltpu.VMEM((heads, rows, HD), f32),
                 pltpu.VMEM((heads, rows, HD), f32),
                 pltpu.VMEM((rows, width_here), bf16),
-                dma((kvc,)), dma((kvc,)), dma((kvc,)), dma((kvc,)),
+                dma, dma((kvc,)), dma((kvc,)), dma((kvc,)), dma((kvc,)),
                 dma((past,)), dma((past,)),
                 dma((past, kvc)), dma((past, kvc)), dma((past, kvc)), dma((past, kvc)),
             ],
             compiler_params=pltpu.CompilerParams(
                 collective_id=0, has_side_effects=True, vmem_limit_bytes=40 << 20
             ),
-        )(queries, keys_values, doc_ids[None])
+        )(
+            pltpu.with_memory_space_constraint(queries, pltpu.HBM),
+            pltpu.with_memory_space_constraint(keys_values, pltpu.HBM),
+            pltpu.with_memory_space_constraint(doc_ids[None], pltpu.HBM),
+        )
 
     return jax.shard_map(
         per_device,

time: 21.8 us -> 18.8 us (0.86)
  local copies, waits for them, and re-layouts: 4.47 us -> 0.97 us
  Pallas kernels: 17.1 us -> 17.6 us
    unnamed x7 -> x1, local copies, waits for them, and re-layouts: 4.47 us -> 0.97 us
    pallas_call x1, Pallas kernels: 17.1 us -> 17.6 us  [per_device(): pl.pallas_call(functools.partial(kernel, n, kvc, share, group_width), out...]
where the time goes in v2:
time: 18.8 us; the launch traced here: 18.6 us
  Pallas kernels  17.6 us (94%)
  local copies, waits for them, and re-layouts  0.97 us (5%)
    pallas_call x1, Pallas kernels, per_device(): pl.pallas_call(functools.partial(kernel, n, kvc, share, group_width), out...  17.6 us
    unnamed x1, local copies, waits for them, and re-layouts  0.97 us

profile of v2, /device:TPU:6, one launch (start us, length us, event | category | flops | bytes accessed | tf_op | source)
XLA Modules:
  0.0 18.6 jit_solution(6460354340027160865)
XLA Ops:
  0.0 17.6 %shard_map.37 = bf16[512,1024]{1,0:T(8,128)(2,1)S(1)} custom-call(bf16[512,1024]{1,0:T(8,128)(2,1)} %q_hbm.1, bf16[2,512,1024]{2,1,0:T(8,128)(2,1)} %kv_hbm.1, s32[1,512]{1,0:T(1,128)} %bitcast.1), custom_call_target="tpu_custom_call" | custom-call | tf_op jit(solution)/shard_map/pallas_call | solution.py:213
  17.6 1.0 %copy.5 = bf16[512,1024]{1,0:T(8,128)(2,1)} copy(bf16[512,1024]{1,0:T(8,128)(2,1)S(1)} %shard_map.37) | data formatting | bytes 2097152

commit v3 on v2

--- a/solution.py
+++ b/solution.py
@@ -9,7 +9,8 @@
 from jax.sharding import PartitionSpec as P
 
 HD = 128
-TILE = 128
+OWN = 256
+REM = 256
 HIDDEN = -1e30
 MESH = pl.DeviceIdType.MESH
 
@@ -23,13 +24,12 @@
 
 
 def kernel(
-    n, kvc, share, group_width, q_hbm, kv_hbm, ids_hbm, out_hbm,
-    q, k_own, v_own, k_in, v_in, ids_own, ids_in, ids_col, bias, weights, acc, top, total, out_buf,
-    ids_sem, q_sem, k_sem, v_sem, out_sem, ids_send, ids_recv, k_send, k_recv, v_send, v_recv,
+    n, kvc, share, group_width, q_hbm, kv_hbm, ids_hbm, out,
+    q, k_own, v_own, k_in, v_in, ids_own, ids_in, ids_col, bias, weights, acc, top, total,
+    ids_sem, q_sem, k_sem, v_sem, ids_send, ids_recv, k_send, k_recv, v_send, v_recv,
 ):
     rows = q_hbm.shape[0]
     heads = kvc * share
-    tiles = rows // TILE
     width = share * HD
     role = lax.axis_index("role")
     first_kv = lax.axis_index("tensor") * heads // group_width
@@ -53,10 +53,6 @@
 
     def v_copy(c):
         return pltpu.make_async_copy(side(1, c), v_own.at[c], v_sem.at[c])
-
-    def out_copy(c):
-        cols = slice(c * width, (c + 1) * width)
-        return pltpu.make_async_copy(out_buf.at[:, cols], out_hbm.at[:, cols], out_sem.at[c])
 
     def remote(src, dst, send, recv, k):
         return pltpu.make_async_remote_copy(
@@ -98,11 +94,11 @@
     def wide(part, times):
         return jnp.concatenate([part] * times, axis=1) if times > 1 else part
 
-    for t in range(tiles):
-        r = slice(t * TILE, (t + 1) * TILE)
-        w = (t + 1) * TILE
-        row_at = lax.broadcasted_iota(jnp.int32, (TILE, w), 0) + t * TILE
-        col_at = lax.broadcasted_iota(jnp.int32, (TILE, w), 1)
+    for t in range(rows // OWN):
+        r = slice(t * OWN, (t + 1) * OWN)
+        w = (t + 1) * OWN
+        row_at = lax.broadcasted_iota(jnp.int32, (OWN, w), 0) + t * OWN
+        col_at = lax.broadcasted_iota(jnp.int32, (OWN, w), 1)
         same = wide(ids_col[r, :], w // HD) == ids_row[:, :w]
         bias[r, :w] = jnp.where(same & (col_at <= row_at), 0.0, HIDDEN)
 
@@ -111,26 +107,26 @@
 
     def own(c, j):
         h = c * share + j
-        for t in range(tiles):
-            r = slice(t * TILE, (t + 1) * TILE)
-            w = (t + 1) * TILE
+        for t in range(rows // OWN):
+            r = slice(t * OWN, (t + 1) * OWN)
+            w = (t + 1) * OWN
             s = dot_t(q[r, head_cols(h)], k_own[c, :w, :]) + bias[r, :w]
             largest = jnp.max(s, axis=1, keepdims=True)
             e = jnp.exp2((s - largest) * rate)
-            top[h, r, :] = jnp.broadcast_to(largest, (TILE, HD))
-            total[h, r, :] = jnp.broadcast_to(jnp.sum(e, axis=1, keepdims=True), (TILE, HD))
+            top[h, r, :] = jnp.broadcast_to(largest, (OWN, HD))
+            total[h, r, :] = jnp.broadcast_to(jnp.sum(e, axis=1, keepdims=True), (OWN, HD))
             acc[h, r, :] = dot(e.astype(jnp.bfloat16), v_own[c, :w, :])
 
     for c in range(kvc):
         q_copy(c).wait()
         k_copy(c).wait()
         v_copy(c).wait()
-        lax.fori_loop(0, share, lambda j, carry: (own(c, j), carry)[1], 0)
+        lax.fori_loop(0, share, lambda j, carry: (own(c, j), carry)[1], 0, unroll=True)
 
     def weigh(k, c, j):
         h = c * share + j
-        for t in range(tiles):
-            r = slice(t * TILE, (t + 1) * TILE)
+        for t in range(rows // REM):
+            r = slice(t * REM, (t + 1) * REM)
             s = dot_t(q[r, head_cols(h)], k_in[k - 1, c]) + bias[r, :]
             before = top[h, r, :]
             largest = jnp.maximum(before, jnp.max(s, axis=1, keepdims=True))
@@ -148,14 +144,14 @@
     def finish_values(k, c, j):
         h = c * share + j
         summed = acc[h] + dot(weights[h], v_in[k - 1, c])
-        out_buf[:, head_cols(h)] = (summed / total[h]).astype(jnp.bfloat16)
+        out[:, head_cols(h)] = (summed / total[h]).astype(jnp.bfloat16)
 
     def finish_own(c, j):
         h = c * share + j
-        out_buf[:, head_cols(h)] = (acc[h] / total[h]).astype(jnp.bfloat16)
+        out[:, head_cols(h)] = (acc[h] / total[h]).astype(jnp.bfloat16)
 
     def each(body):
-        lax.fori_loop(0, share, lambda j, carry: (body(j), carry)[1], 0)
+        lax.fori_loop(0, share, lambda j, carry: (body(j), carry)[1], 0, unroll=True)
 
     for k in range(1, n):
 
@@ -177,16 +173,12 @@
                 @pl.when(role == k)
                 def _():
                     each(functools.partial(finish_values, k, c))
-                    out_copy(c).start()
 
     @pl.when(role == 0)
     def _():
         for c in range(kvc):
             each(functools.partial(finish_own, c))
-            out_copy(c).start()
-
-    for c in range(kvc):
-        out_copy(c).wait()
+
     for k in range(1, n):
 
         @pl.when(role + k < n)
@@ -218,7 +210,7 @@
                 pl.BlockSpec(memory_space=pl.ANY),
                 pl.BlockSpec(memory_space=pl.ANY),
             ],
-            out_specs=pl.BlockSpec(memory_space=pl.ANY),
+            out_specs=pl.BlockSpec(memory_space=pltpu.VMEM),
             scratch_shapes=[
                 pltpu.VMEM((rows, width_here), bf16),
                 pltpu.VMEM((kvc, rows, HD), bf16),
@@ -233,8 +225,7 @@
                 pltpu.VMEM((heads, rows, HD), f32),
                 pltpu.VMEM((heads, rows, HD), f32),
                 pltpu.VMEM((heads, rows, HD), f32),
-                pltpu.VMEM((rows, width_here), bf16),
-                dma, dma((kvc,)), dma((kvc,)), dma((kvc,)), dma((kvc,)),
+                dma, dma((kvc,)), dma((kvc,)), dma((kvc,)),
                 dma((past,)), dma((past,)),
                 dma((past, kvc)), dma((past, kvc)), dma((past, kvc)), dma((past, kvc)),
             ],

time: 18.8 us -> 15.9 us (0.85)
  Pallas kernels: 17.6 us -> 14.8 us
    pallas_call x1, Pallas kernels: 17.6 us -> 14.8 us  [per_device(): pl.pallas_call(functools.partial(kernel, n, kvc, share, group_width), out...]
where the time goes in v3:
time: 15.9 us; the launch traced here: 15.8 us
  Pallas kernels  14.8 us (93%)
  local copies, waits for them, and re-layouts  0.97 us (6%)
    pallas_call x1, Pallas kernels, per_device(): pl.pallas_call(functools.partial(kernel, n, kvc, share, group_width), out...  14.8 us
    unnamed x1, local copies, waits for them, and re-layouts  0.97 us

profile of v3, /device:TPU:6, one launch (start us, length us, event | category | flops | bytes accessed | tf_op | source)
XLA Modules:
  0.0 15.8 jit_solution(12090880019200982654)
XLA Ops:
  0.0 14.8 %shard_map.37 = bf16[512,1024]{1,0:T(8,128)(2,1)S(1)} custom-call(bf16[512,1024]{1,0:T(8,128)(2,1)} %q_hbm.1, bf16[2,512,1024]{2,1,0:T(8,128)(2,1)} %kv_hbm.1, s32[1,512]{1,0:T(1,128)} %bitcast.1), custom_call_target="tpu_custom_call" | custom-call | tf_op jit(solution)/shard_map/pallas_call | solution.py:205
  14.8 1.0 %copy.5 = bf16[512,1024]{1,0:T(8,128)(2,1)} copy(bf16[512,1024]{1,0:T(8,128)(2,1)S(1)} %shard_map.37) | data formatting | bytes 2097152

commit v4 on v3

--- a/solution.py
+++ b/solution.py
@@ -66,8 +66,16 @@
     def k_remote(k, c):
         return remote(side(0, c), k_in.at[k - 1, c], k_send.at[k - 1, c], k_recv.at[k - 1, c], k)
 
-    def v_remote(k, c):
-        return remote(side(1, c), v_in.at[k - 1, c], v_send.at[k - 1, c], v_recv.at[k - 1, c], k)
+    half = rows // 2
+
+    def v_remote(k, c, i):
+        part = pl.ds(i * half, half)
+        cols = pl.ds(pl.multiple_of((first_kv + c) * HD, HD), HD)
+        at = 2 * c + i
+        return remote(
+            kv_hbm.at[1, part, cols], v_in.at[k - 1, c, part],
+            v_send.at[k - 1, at], v_recv.at[k - 1, at], k,
+        )
 
     ids_copy = pltpu.make_async_copy(ids_hbm, ids_own, ids_sem)
     ids_copy.start()
@@ -85,7 +93,8 @@
             for c in range(kvc):
                 k_remote(k, c).start()
             for c in range(kvc):
-                v_remote(k, c).start()
+                for i in range(2):
+                    v_remote(k, c, i).start()
 
     ids_copy.wait()
     ids_row = ids_own[...]
@@ -139,11 +148,15 @@
 
     def add_values(k, c, j):
         h = c * share + j
-        acc[h] = acc[h] + dot(weights[h], v_in[k - 1, c])
+        acc[h] = acc[h] + dot(weights[h, :, :half], v_in[k - 1, c, :half])
+
+    def add_rest(k, c, j):
+        h = c * share + j
+        acc[h] = acc[h] + dot(weights[h, :, half:], v_in[k - 1, c, half:])
 
     def finish_values(k, c, j):
         h = c * share + j
-        summed = acc[h] + dot(weights[h], v_in[k - 1, c])
+        summed = acc[h] + dot(weights[h, :, half:], v_in[k - 1, c, half:])
         out[:, head_cols(h)] = (summed / total[h]).astype(jnp.bfloat16)
 
     def finish_own(c, j):
@@ -164,11 +177,13 @@
                 k_remote(k, c).wait_recv()
                 each(functools.partial(weigh, k, c))
             for c in range(kvc):
-                v_remote(k, c).wait_recv()
+                v_remote(k, c, 0).wait_recv()
+                each(functools.partial(add_values, k, c))
+                v_remote(k, c, 1).wait_recv()
 
                 @pl.when(role > k)
                 def _():
-                    each(functools.partial(add_values, k, c))
+                    each(functools.partial(add_rest, k, c))
 
                 @pl.when(role == k)
                 def _():
@@ -186,7 +201,8 @@
             ids_remote(k).wait_send()
             for c in range(kvc):
                 k_remote(k, c).wait_send()
-                v_remote(k, c).wait_send()
+                for i in range(2):
+                    v_remote(k, c, i).wait_send()
 
 
 def solution(mesh):
@@ -227,7 +243,7 @@
                 pltpu.VMEM((heads, rows, HD), f32),
                 dma, dma((kvc,)), dma((kvc,)), dma((kvc,)),
                 dma((past,)), dma((past,)),
-                dma((past, kvc)), dma((past, kvc)), dma((past, kvc)), dma((past, kvc)),
+                dma((past, kvc)), dma((past, kvc)), dma((past, 2 * kvc)), dma((past, 2 * kvc)),
             ],
             compiler_params=pltpu.CompilerParams(
                 collective_id=0, has_side_effects=True, vmem_limit_bytes=40 << 20

time: 15.9 us -> 15.8 us (level)
  Pallas kernels: 14.8 us -> 14.6 us
    pallas_call x1, Pallas kernels: 14.8 us -> 14.6 us  [per_device(): pl.pallas_call(functools.partial(kernel, n, kvc, share, group_width), out...]
where the time goes in v4:
time: 15.8 us; the launch traced here: 15.5 us
  Pallas kernels  14.6 us (92%)
  local copies, waits for them, and re-layouts  0.97 us (6%)
    pallas_call x1, Pallas kernels, per_device(): pl.pallas_call(functools.partial(kernel, n, kvc, share, group_width), out...  14.6 us
    unnamed x1, local copies, waits for them, and re-layouts  0.97 us

profile of v4, /device:TPU:6, one launch (start us, length us, event | category | flops | bytes accessed | tf_op | source)
XLA Modules:
  0.0 15.5 jit_solution(10161117784126390696)
XLA Ops:
  0.0 14.6 %shard_map.37 = bf16[512,1024]{1,0:T(8,128)(2,1)S(1)} custom-call(bf16[512,1024]{1,0:T(8,128)(2,1)} %q_hbm.1, bf16[2,512,1024]{2,1,0:T(8,128)(2,1)} %kv_hbm.1, s32[1,512]{1,0:T(1,128)} %bitcast.1), custom_call_target="tpu_custom_call" | custom-call | tf_op jit(solution)/shard_map/pallas_call | solution.py:221
  14.6 1.0 %copy.5 = bf16[512,1024]{1,0:T(8,128)(2,1)} copy(bf16[512,1024]{1,0:T(8,128)(2,1)S(1)} %shard_map.37) | data formatting | bytes 2097152
